TPU v7x, 256 devices: a whole 4x4x8 slice. The times are simulated.
256 devices in a mesh: view: 16 (over z, core), blk: 16 (over y, x).
Axes of the slice: x: 4, y: 4, z: 8, core: 2. Of those that a mesh axis runs over, the one named last changes fastest.
Arguments:
- estimate: float32 [256, 128, 128], P('blk'), may hold values from 0.5 to 2
- images: bfloat16 [16, 256, 64, 128], P('view', 'blk'), may hold values from 0.5 to 2
- point_spread: float32 [8, 9, 7, 25], replicated, may hold values from 0.01 to 1
- covered: int32 [8, 16, 4], P(None, 'blk'), may hold values from 0 to 1, as said below
Outputs:
- estimate_next: float32 [256, 128, 128], P('blk')
Inputs may be any that keep to these rules, and one draw needn't show every extreme that they name: For each view and each block layer along the first dimension, the covered blocks are consecutive along the second dimension and at most 3; for every view some block layer has exactly 3.
All inputs are finite; a program needn't handle non-finite values.
Results may differ from a plain program's by a relative error of at most 0.0003.
Values may be sent and summed in bfloat16 or wider, within the bound.
A program may use at most 64 MiB of HBM per device.

v0:
```python
import jax
import jax.numpy as jnp
from jax import lax
from jax.sharding import PartitionSpec as P

BY = 32


def with_halo(cells, sides, width):
    for axis, dim in sides:
        count = lax.axis_size(axis)
        ends = count - 1
        head = lax.slice_in_dim(cells, 0, width, axis=dim)
        tail = lax.slice_in_dim(cells, cells.shape[dim] - width, cells.shape[dim], axis=dim)
        cells = jnp.concatenate(
            [
                lax.ppermute(tail, axis, [(i, (i + 1) % count) for i in range(ends)]),
                cells,
                lax.ppermute(head, axis, [((i + 1) % count, i) for i in range(ends)]),
            ],
            axis=dim,
        )
    return cells


def swapped(block, axis, stride):
    count = lax.axis_size(axis)
    route = []
    for low in range(count):
        high = low | 1 << stride
        if high != low and high < count:
            route += [(low, high), (high, low)]
    return lax.ppermute(block, axis, route)


def merged(part, axis, combine):
    gathered = lax.all_gather(part, axis)

    def take(source):
        return lax.dynamic_index_in_dim(gathered, source, 0, False)

    return lax.fori_loop(
        1, lax.axis_size(axis), lambda source, state: combine(state, take(source)), take(0)
    )


def band_table(kernel, depth):
    taps_x, taps_y, taps_z = kernel.shape
    rim_z = (taps_z - 1) // 2
    shape_three = (taps_z, depth, depth)
    offset = lax.broadcasted_iota(jnp.int32, shape_three, 1) - lax.broadcasted_iota(
        jnp.int32, shape_three, 2
    )
    onehot = (offset + rim_z == lax.broadcasted_iota(jnp.int32, shape_three, 0)).astype(
        jnp.bfloat16
    )
    banded = jnp.einsum("abt,tpz->abpz", kernel, onehot, preferred_element_type=jnp.float32).astype(
        jnp.bfloat16
    )
    return banded.reshape(taps_x, taps_y * depth, depth)


def convolve(padded_part, banded, rows_x, rows_y):
    taps_x = padded_part.shape[0] - rows_x + 1
    taps_y = padded_part.shape[1] - rows_y + 1
    columns = jnp.concatenate(
        [padded_part[:, step_y : step_y + rows_y, :] for step_y in range(taps_y)], axis=2
    )
    output = None
    for shift_x in range(taps_x):
        partial_sum = jnp.dot(
            columns[shift_x : shift_x + rows_x].reshape(rows_x * rows_y, -1),
            banded[shift_x],
            preferred_element_type=jnp.float32,
        )
        output = partial_sum if output is None else output + partial_sum
    return output.reshape(rows_x, rows_y, -1)


def local(estimate, images, point_spread, covered):
    slab_x, width_y, depth = estimate.shape
    share_w = images.shape[2]
    view_count, taps_x, taps_y, taps_z = point_spread.shape
    rim_x, rim_y, rim_z = ((taps_x - 1) // 2, (taps_y - 1) // 2, (taps_z - 1) // 2)
    shares = width_y // share_w
    share_blocks = share_w // BY
    group = lax.axis_index("view")
    view_id = group // shares
    part = group % shares
    y_start = part * share_w
    source = estimate.astype(jnp.bfloat16)
    rimmed = with_halo(source, (("blk", 0),), rim_x)
    padded = jnp.pad(rimmed, ((0, 0), (rim_y, rim_y), (0, 0)))
    spread = lax.dynamic_index_in_dim(point_spread, view_id, 0, keepdims=False)
    kernel = (spread / jnp.sum(spread)).astype(jnp.bfloat16)
    forward = band_table(kernel, depth)
    backward = band_table(kernel[::-1, ::-1, ::-1], depth)
    coverage_row = lax.dynamic_index_in_dim(covered[:, 0, :], view_id, 0, keepdims=False) > 0
    share_cover = lax.dynamic_slice_in_dim(coverage_row, part * share_blocks, share_blocks)
    cell_cover = jnp.repeat(share_cover, BY)[None, :, None]
    image = images[0]
    region = lax.dynamic_slice(
        padded, (0, y_start, 0), (slab_x + 2 * rim_x, share_w + 2 * rim_y, depth)
    )
    blurred = convolve(region, forward, slab_x, share_w)
    quotient = jnp.where(cell_cover, image.astype(jnp.float32) / blurred, 0.0).astype(jnp.bfloat16)
    rim_zeros = jnp.zeros((slab_x, rim_y, depth), jnp.bfloat16)
    edge_rows = jnp.where(part == 0, quotient[:, share_w - rim_y :, :], quotient[:, :rim_y, :])
    partner = swapped(edge_rows, "view", 0)
    lower_rim = jnp.where(part > 0, partner, rim_zeros)
    upper_rim = jnp.where(part < shares - 1, partner, rim_zeros)
    extended = jnp.concatenate([lower_rim, quotient, upper_rim], axis=1)
    quotient_rimmed = with_halo(extended, (("blk", 0),), rim_x)
    correction = convolve(quotient_rimmed, backward, slab_x, share_w)
    share_factor = jnp.where(cell_cover, correction, 1.0)
    n_view = lax.axis_size("view")
    step_x = slab_x // n_view
    rows = share_factor.reshape(n_view, step_x, share_w, depth)
    got = lax.all_to_all(rows, "view", 0, 0)
    got = got.reshape(n_view // shares, shares, step_x, share_w, depth)
    product_rows = jnp.prod(got, axis=0)
    product_rows = jnp.transpose(product_rows, (1, 0, 2, 3)).reshape(step_x, width_y, depth)
    mine = lax.dynamic_slice_in_dim(estimate, group * step_x, step_x, axis=0)
    return lax.all_gather(mine * product_rows, "view", axis=0, tiled=True)


def solution(mesh):
    in_specs = (P("blk", None, None), P("view", "blk", None, None), P(), P(None, "blk", None))
    out_specs = P("blk", None, None)
    return jax.shard_map(local, mesh=mesh, in_specs=in_specs, out_specs=out_specs, check_vma=False)
```

profile of v0, /device:TPU:1, one launch (start us, length us, event | category | flops | bytes accessed | tf_op | source)
XLA Modules:
  0.0 128.2 jit_solution(17272270914108477657)
XLA Ops:
  6.5 1.3 %convert_element_type.30 = bf16[16,128,128]{2,1,0:T(8,128)(2,1)S(1)} convert(f32[16,128,128]{2,1,0:T(8,128)} %param.4) | non-fusion elementwise | flops 262144 | bytes 1572864 | tf_op jit(solution)/shard_map/convert_element_type | solution.py:91
  7.9 4.0 %collective-permute-start = (bf16[4,128,128]{2,1,0:T(8,128)(2,1)S(1)}, bf16[4,128,128]{2,1,0:T(8,128)(2,1)S(1)}, u32[]{:S(2)}, u32[]{:S(2)}) collective-permute-start(bf16[4,128,128]{2,1,0:T(8,128)(2,1)S(1)} %get-tuple-element.44), channel_id=1, source_target_pairs={{0,1},{1,2},{2,3},{3,4},{4,5},{5,6},{6,7},{7,8},{8,9},{9,10},{10,1... | collective-permute-start | bytes 393224 | tf_op jit(solution)/shard_map/ppermute | solution.py:17
  11.8 1.3 %collective-permute-start.1 = (bf16[4,128,128]{2,1,0:T(8,128)(2,1)S(1)}, bf16[4,128,128]{2,1,0:T(8,128)(2,1)S(1)}, u32[]{:S(2)}, u32[]{:S(2)}) collective-permute-start(bf16[4,128,128]{2,1,0:T(8,128)(2,1)S(1)} %get-tuple-element.43), channel_id=1, source_target_pairs={{1,0},{2,1},{3,2},{4,3},{5,4},{6,5},{7,6},{8,7},{9,8},{10,9},{11,1... | collective-permute-start | bytes 393224 | tf_op jit(solution)/shard_map/ppermute | solution.py:19
  13.2 1.6 %fusion.30 = (f32[]{:T(128)}, f32[1,9,7,25]{3,0,2,1:T(1,128)S(1)}) fusion(f32[8,9,7,25]{3,0,2,1:T(8,128)} %param.6, s32[]{:T(128)S(6)} %select_n.62), kind=kLoop, calls=%fused_computation.73 | loop fusion | flops 1574 | bytes 12608 | tf_op jit(solution)/shard_map/reduce_sum | solution.py:95
  14.8 1.5 %fusion.5 = bf16[9,7,128,128]{3,1,2,0:T(8,128)(2,1)S(1)} fusion(f32[1,9,7,25]{3,0,2,1:T(1,128)S(1)} %get-tuple-element.6, f32[]{:T(128)} %get-tuple-element.5), kind=kOutput, calls=%fused_computation.4 | convolution fusion | flops 53873744 | bytes 2070688 | tf_op jit(solution)/shard_map/abt,tpz->abpz/dot_general | solution.py:57
  16.3 0.2 fusion.34
  16.9 0.4 copy-done.1
  17.3 0.1 dynamic-slice_compare_fusion
  17.3 0.1 dynamic-slice_reduce_fusion
  17.5 0.1 broadcast_in_dim.28
  17.5 0.1 broadcast_in_dim.29
  17.6 0.7 fusion.29
  18.3 0.1 rev.3
  18.4 0.3 fusion.20
  18.8 0.1 slice_dynamic-update-slice_fusion.13
  18.9 0.2 slice_dynamic-update-slice_fusion.12
  19.0 0.2 slice_dynamic-update-slice_fusion.11
  19.2 0.2 slice_dynamic-update-slice_fusion.10
  19.4 0.2 slice_dynamic-update-slice_fusion.9
  19.6 0.2 slice_dynamic-update-slice_fusion.8
  19.7 0.2 slice_dynamic-update-slice_fusion.7
  19.9 3.2 %fusion.32 = (bf16[16,64,896]{2,1,0:T(8,128)(2,1)S(1)}, bf16[16,64,896]{2,1,0:T(8,128)(2,1)S(1)}, bf16[16,64,896]{2,1,0:T(8,128)(2,1)S(1)}, bf16[16,64,896]{2,1,...) fusion(bf16[24,64,896]{2,1,0:T(8,128)(2,1)S(1)} %slice_dynamic-, ...), kind=kLoop, calls=%fused_computation.75 | loop fusion | bytes 33030144 | tf_op jit(solution)/shard_map/slice | solution.py:72
  23.1 0.6 fusion.36
  23.8 0.7 convolution_add_fusion.15
  24.4 0.6 convolution_add_fusion.14
  25.1 0.6 convolution_add_fusion.13
  25.7 0.6 convolution_add_fusion.12
  26.4 0.6 convolution_add_fusion.11
  27.0 0.6 convolution_add_fusion.10
  27.7 0.6 convolution_add_fusion.9
  28.4 0.7 convolution_add_fusion.8
  29.0 0.3 copy-done
  29.3 0.1 fusion.17
  29.5 1.3 %collective-permute-start.2 = (bf16[16,3,128]{2,1,0:T(4,128)(2,1)S(1)}, bf16[16,3,128]{2,1,0:T(4,128)(2,1)S(1)}, u32[]{:S(2)}, u32[]{:S(2)}) collective-permute-start(bf16[16,3,128]{2,1,0:T(4,128)(2,1)S(1)} %slice_select_fusion), channel_id=1, source_target_pairs={{0,16},{16,0},{32,48},{48,32},{64,80},{80,64},{96,112},{112,96},{1... | collective-permute-start | bytes 36872 | tf_op jit(solution)/shard_map/ppermute | solution.py:33
  30.8 0.9 fusion.8
  31.7 0.1 pad_maximum_fusion.3
  31.8 1.3 %collective-permute-start.4 = (bf16[4,70,128]{2,1,0:T(8,128)(2,1)S(1)}, bf16[4,70,128]{2,1,0:T(8,128)(2,1)S(1)}, u32[]{:S(2)}, u32[]{:S(2)}) collective-permute-start(bf16[4,70,128]{2,1,0:T(8,128)(2,1)S(1)} %get-tuple-element.46), channel_id=1, source_target_pairs={{1,0},{2,1},{3,2},{4,3},{5,4},{6,5},{7,6},{8,7},{9,8},{10,9},{11,1... | collective-permute-start | bytes 215048 | tf_op jit(solution)/shard_map/ppermute | solution.py:19
  33.1 4.8 %collective-permute-start.3 = (bf16[4,70,128]{2,1,0:T(8,128)(2,1)S(1)}, bf16[4,70,128]{2,1,0:T(8,128)(2,1)S(1)}, u32[]{:S(2)}, u32[]{:S(2)}) collective-permute-start(bf16[4,70,128]{2,1,0:T(8,128)(2,1)S(1)} %get-tuple-element.45), channel_id=1, source_target_pairs={{0,1},{1,2},{2,3},{3,4},{4,5},{5,6},{6,7},{7,8},{8,9},{9,10},{10,1... | collective-permute-start | bytes 215048 | tf_op jit(solution)/shard_map/ppermute | solution.py:17
  37.9 0.2 fusion.33
  38.4 0.6 collective-permute-done.3
  39.1 0.1 pad_maximum_fusion
  39.2 0.1 slice_dynamic-update-slice_fusion.6
  39.3 0.2 slice_dynamic-update-slice_fusion.5
  39.5 0.2 slice_dynamic-update-slice_fusion.4
  39.6 0.2 slice_dynamic-update-slice_fusion.3
  39.8 0.2 slice_dynamic-update-slice_fusion.2
  40.0 0.2 slice_dynamic-update-slice_fusion.1
  40.2 0.2 slice_dynamic-update-slice_fusion
  40.3 3.2 %fusion.31 = (bf16[16,64,896]{2,1,0:T(8,128)(2,1)S(1)}, bf16[16,64,896]{2,1,0:T(8,128)(2,1)S(1)}, bf16[16,64,896]{2,1,0:T(8,128)(2,1)S(1)}, bf16[16,64,896]{2,1,...) fusion(bf16[24,64,896]{2,1,0:T(8,128)(2,1)S(1)} %slice_dynamic-, ...), kind=kLoop, calls=%fused_computation.74 | loop fusion | bytes 33030144 | tf_op jit(solution)/shard_map/slice | solution.py:72
  43.5 0.6 fusion.37
  44.2 0.7 convolution_add_fusion.7
  44.8 0.6 convolution_add_fusion.6
  45.5 0.6 convolution_add_fusion.5
  46.1 0.6 convolution_add_fusion.4
  46.8 0.6 convolution_add_fusion.3
  47.5 0.6 convolution_add_fusion.2
  48.1 0.6 convolution_add_fusion.1
  48.8 0.6 convolution_add_fusion
  49.4 0.9 broadcast_select_fusion
  50.3 9.6 %all-to-all-start = ((f32[16,1,64,128]{3,2,1,0:T(8,128)}), f32[16,1,64,128]{3,2,1,0:T(8,128)S(1)}, u32[]{:S(2)}, u32[]{:S(2)}) async-start(f32[16,1,64,128]{3,2,1,0:T(8,128)} %broadcast_select_fusion), calls=%async_computation | async-start | bytes 1048576 | tf_op jit(solution)/shard_map/all_to_all | solution.py:119
  60.0 17.3 %all-to-all-done = f32[16,1,64,128]{3,2,1,0:T(8,128)S(1)} async-done(((f32[16,1,64,128]{3,2,1,0:T(8,128)}), f32[16,1,64,128]{3,2,1,0:T(8,128)S(1)}, u32[]{:S(2)}, u32[]{:S(2)}) %all-to-all-start) | async-done | bytes 524320 | tf_op jit(solution)/shard_map/all_to_all | solution.py:119
  77.3 1.5 %bitcast_multiply_fusion = f32[1,128,128]{2,1,0:T(8,128)} fusion(f32[16,128,128]{2,1,0:T(8,128)} %param.4, s32[]{:T(128)S(6)} %select_n.60, f32[1,128,128]{2,1,0:T(8,128)S(1)} %bitcast.144), kind=kLoop, calls=%fused_computation.59 | loop fusion | flops 16384 | bytes 196612 | tf_op jit(solution)/shard_map/mul | solution.py:124
  78.8 40.3 %all-gather.2.cloned.1.call-done = f32[16,128,128]{2,1,0:T(8,128)} async-done(((f32[1,128,128]{2,1,0:T(8,128)}), f32[16,128,128]{2,1,0:T(8,128)}) %all-gather.2.cloned.1.call-update) | async-done | bytes 1048592 | tf_op jit(solution)/shard_map/all_gather | solution.py:124
  119.1 2.3 %copy.70 = f32[16,128,128]{2,1,0:T(8,128)} copy(f32[16,128,128]{2,1,0:T(8,128)} %all-gather.2.cloned.1.call-done) | data formatting | bytes 2097152
  (30 shorter events, 0.8 us)
Async XLA Ops:
  7.9 10.5 %collective-permute-start = (bf16[4,128,128]{2,1,0:T(8,128)(2,1)S(1)}, bf16[4,128,128]{2,1,0:T(8,128)(2,1)S(1)}, u32[]{:S(2)}, u32[]{:S(2)}) collective-permute-start(bf16[4,128,128]{2,1,0:T(8,128)(2,1)S(1)} %get-tuple-element.44), channel_id=1, source_target_pairs={{0,1},{1,2},{2,3},{3,4},{4,5},{5,6},{6,7},{7,8},{8,9},{9,10},{10,1... | collective-permute-start | bytes 393224 | tf_op jit(solution)/shard_map/ppermute | solution.py:17
  11.8 6.6 %collective-permute-start.1 = (bf16[4,128,128]{2,1,0:T(8,128)(2,1)S(1)}, bf16[4,128,128]{2,1,0:T(8,128)(2,1)S(1)}, u32[]{:S(2)}, u32[]{:S(2)}) collective-permute-start(bf16[4,128,128]{2,1,0:T(8,128)(2,1)S(1)} %get-tuple-element.43), channel_id=1, source_target_pairs={{1,0},{2,1},{3,2},{4,3},{5,4},{6,5},{7,6},{8,7},{9,8},{10,9},{11,1... | collective-permute-start | bytes 393224 | tf_op jit(solution)/shard_map/ppermute | solution.py:19
  16.6 0.7 copy-start.1
  28.3 1.0 copy-start
  29.5 2.2 %collective-permute-start.2 = (bf16[16,3,128]{2,1,0:T(4,128)(2,1)S(1)}, bf16[16,3,128]{2,1,0:T(4,128)(2,1)S(1)}, u32[]{:S(2)}, u32[]{:S(2)}) collective-permute-start(bf16[16,3,128]{2,1,0:T(4,128)(2,1)S(1)} %slice_select_fusion), channel_id=1, source_target_pairs={{0,16},{16,0},{32,48},{48,32},{64,80},{80,64},{96,112},{112,96},{1... | collective-permute-start | bytes 36872 | tf_op jit(solution)/shard_map/ppermute | solution.py:33
  31.8 6.7 %collective-permute-start.4 = (bf16[4,70,128]{2,1,0:T(8,128)(2,1)S(1)}, bf16[4,70,128]{2,1,0:T(8,128)(2,1)S(1)}, u32[]{:S(2)}, u32[]{:S(2)}) collective-permute-start(bf16[4,70,128]{2,1,0:T(8,128)(2,1)S(1)} %get-tuple-element.46), channel_id=1, source_target_pairs={{1,0},{2,1},{3,2},{4,3},{5,4},{6,5},{7,6},{8,7},{9,8},{10,9},{11,1... | collective-permute-start | bytes 215048 | tf_op jit(solution)/shard_map/ppermute | solution.py:19
  33.1 6.0 %collective-permute-start.3 = (bf16[4,70,128]{2,1,0:T(8,128)(2,1)S(1)}, bf16[4,70,128]{2,1,0:T(8,128)(2,1)S(1)}, u32[]{:S(2)}, u32[]{:S(2)}) collective-permute-start(bf16[4,70,128]{2,1,0:T(8,128)(2,1)S(1)} %get-tuple-element.45), channel_id=1, source_target_pairs={{0,1},{1,2},{2,3},{3,4},{4,5},{5,6},{6,7},{7,8},{8,9},{9,10},{10,1... | collective-permute-start | bytes 215048 | tf_op jit(solution)/shard_map/ppermute | solution.py:17
  50.3 26.9 %all-to-all-start = ((f32[16,1,64,128]{3,2,1,0:T(8,128)}), f32[16,1,64,128]{3,2,1,0:T(8,128)S(1)}, u32[]{:S(2)}, u32[]{:S(2)}) async-start(f32[16,1,64,128]{3,2,1,0:T(8,128)} %broadcast_select_fusion), calls=%async_computation | async-start | bytes 1048576 | tf_op jit(solution)/shard_map/all_to_all | solution.py:119
  60.0 59.1 %all-gather.2.cloned.1.call-start = ((), (), s32[]{:S(2)}) async-start(), calls=%async_computation.1 | async-start | bytes 1114112 | tf_op jit(solution)/shard_map/all_gather | solution.py:124
Sparse Core Ops, SparseCore 0:
  78.9 40.0 all-gather.1
where the time goes:
time: 129 us; the launch traced here: 128 us
  waiting for transfers between devices  58.2 us (45%)
  starting transfers between devices  22.3 us (17%)
  matrix products  14 us (11%)
  between operations  14 us (11%)
  local copies, waits for them, and re-layouts  12.9 us (10%)
  other arithmetic  6.78 us (5%)
    all_gather x1, waiting for transfers between devices, local(): return lax.all_gather(mine * product_rows, 'view', axis=0, tiled=True)  40.3 us
    all_to_all x1, waiting for transfers between devices, local(): got = lax.all_to_all(rows, 'view', 0, 0)  17.3 us
    dot_general x18, matrix products, convolve(): jnp.dot(columns[shift_x:shift_x + rows_x].reshape(rows_x * rows_y, -1), b...  11.7 us
    all_to_all x1, starting transfers between devices, local(): got = lax.all_to_all(rows, 'view', 0, 0)  9.63 us
    ppermute x2, starting transfers between devices, with_halo(): lax.ppermute(tail, axis, [(i, (i + 1) % count) for i in range(ends)])  8.75 us
    slice x2, local copies, waits for them, and re-layouts, convolve(): columns[shift_x:shift_x + rows_x].reshape(rows_x * rows_y, -1)  6.38 us
    unnamed x17, local copies, waits for them, and re-layouts  4.82 us
    ppermute x2, starting transfers between devices, with_halo(): lax.ppermute(head, axis, [((i + 1) % count, i) for i in range(ends)])  2.58 us
  transfers between devices with their start and end apart: 7, of which 3 were waited for; matrix products, arithmetic and copies ran while one was open for 5% of the time, Pallas kernels for 0%

commit v1 on v0

--- a/solution.py
+++ b/solution.py
@@ -4,6 +4,12 @@
 from jax.sharding import PartitionSpec as P
 
 BY = 32
+
+
+def compute_ratios(payload):
+    q_next = jnp.concatenate([payload for _ in range(lax.axis_size("view"))], axis=0)
+    piece_out = lax.all_to_all(q_next, axis_name="view", concat_axis=0, split_axis=0, tiled=True)
+    return piece_out
 
 
 def with_halo(cells, sides, width):
@@ -121,7 +127,7 @@
     product_rows = jnp.prod(got, axis=0)
     product_rows = jnp.transpose(product_rows, (1, 0, 2, 3)).reshape(step_x, width_y, depth)
     mine = lax.dynamic_slice_in_dim(estimate, group * step_x, step_x, axis=0)
-    return lax.all_gather(mine * product_rows, "view", axis=0, tiled=True)
+    return compute_ratios(mine * product_rows)
 
 
 def solution(mesh):

time: 129 us -> 110 us (0.85)
  the two profiles are of different devices: /device:TPU:1 before, /device:TPU:25 now
where the time goes in v1:
time: 110 us
  blocking collectives  31.3 us (28%)
  starting transfers between devices  24.4 us (22%)
  waiting for transfers between devices  21.9 us (20%)
  matrix products  14 us (13%)
  local copies, waits for them, and re-layouts  11.7 us (11%)
  other arithmetic  6.15 us (6%)
    all_to_all x1, blocking collectives, compute_ratios(): lax.all_to_all(q_next, axis_name='view', concat_axis=0, split_axis=0, til...  31.3 us
    all_to_all x1, waiting for transfers between devices, local(): got = lax.all_to_all(rows, 'view', 0, 0)  17.3 us
    dot_general x18, matrix products, convolve(): jnp.dot(columns[shift_x:shift_x + rows_x].reshape(rows_x * rows_y, -1), b...  11.6 us
    all_to_all x1, starting transfers between devices, local(): got = lax.all_to_all(rows, 'view', 0, 0)  10.2 us
    ppermute x2, starting transfers between devices, with_halo(): lax.ppermute(head, axis, [((i + 1) % count, i) for i in range(ends)])  7.67 us
    slice x2, local copies, waits for them, and re-layouts, convolve(): columns[shift_x:shift_x + rows_x].reshape(rows_x * rows_y, -1)  6.38 us
    ppermute x2, starting transfers between devices, with_halo(): lax.ppermute(tail, axis, [(i, (i + 1) % count) for i in range(ends)])  5.22 us
    ppermute x2, waiting for transfers between devices, with_halo(): lax.ppermute(tail, axis, [(i, (i + 1) % count) for i in range(ends)])  4.54 us
  transfers between devices with their start and end apart: 6, of which 2 were waited for; matrix products, arithmetic and copies ran while one was open for 6% of the time, Pallas kernels for 0%

profile of v1, /device:TPU:25, one launch (start us, length us, event | category | flops | bytes accessed | tf_op | source)
XLA Modules:
  0.0 110.0 jit_solution(11583578486269500536)
XLA Ops:
  0.0 1.3 %convert_element_type.30 = bf16[16,128,128]{2,1,0:T(8,128)(2,1)S(1)} convert(f32[16,128,128]{2,1,0:T(8,128)} %param.4) | non-fusion elementwise | flops 262144 | bytes 1572864 | tf_op jit(solution)/shard_map/convert_element_type | solution.py:97
  1.3 3.1 %collective-permute-start = (bf16[4,128,128]{2,1,0:T(8,128)(2,1)S(1)}, bf16[4,128,128]{2,1,0:T(8,128)(2,1)S(1)}, u32[]{:S(2)}, u32[]{:S(2)}) collective-permute-start(bf16[4,128,128]{2,1,0:T(8,128)(2,1)S(1)} %get-tuple-element.44), channel_id=1, source_target_pairs={{0,1},{1,2},{2,3},{3,4},{4,5},{5,6},{6,7},{7,8},{8,9},{9,10},{10,1... | collective-permute-start | bytes 393224 | tf_op jit(solution)/shard_map/ppermute | solution.py:23
  4.5 4.3 %collective-permute-start.1 = (bf16[4,128,128]{2,1,0:T(8,128)(2,1)S(1)}, bf16[4,128,128]{2,1,0:T(8,128)(2,1)S(1)}, u32[]{:S(2)}, u32[]{:S(2)}) collective-permute-start(bf16[4,128,128]{2,1,0:T(8,128)(2,1)S(1)} %get-tuple-element.43), channel_id=1, source_target_pairs={{1,0},{2,1},{3,2},{4,3},{5,4},{6,5},{7,6},{8,7},{9,8},{10,9},{11,1... | collective-permute-start | bytes 393224 | tf_op jit(solution)/shard_map/ppermute | solution.py:25
  8.8 1.6 %fusion.31 = (f32[]{:T(128)}, f32[1,9,7,25]{3,0,2,1:T(1,128)S(1)}) fusion(f32[8,9,7,25]{3,0,2,1:T(8,128)} %param.6, s32[]{:T(128)S(6)} %select_n.62), kind=kLoop, calls=%fused_computation.74 | loop fusion | flops 1574 | bytes 12608 | tf_op jit(solution)/shard_map/reduce_sum | solution.py:101
  10.4 1.5 %fusion.5 = bf16[9,7,128,128]{3,1,2,0:T(8,128)(2,1)S(1)} fusion(f32[1,9,7,25]{3,0,2,1:T(1,128)S(1)} %get-tuple-element.6, f32[]{:T(128)} %get-tuple-element.5), kind=kOutput, calls=%fused_computation.4 | convolution fusion | flops 53873744 | bytes 2070688 | tf_op jit(solution)/shard_map/abt,tpz->abpz/dot_general | solution.py:63
  11.9 0.2 fusion.35
  12.5 0.4 copy-done.1
  12.9 0.1 dynamic-slice_compare_fusion
  12.9 0.1 dynamic-slice_reduce_fusion
  13.1 0.1 broadcast_in_dim.28
  13.1 0.1 broadcast_in_dim.29
  13.2 0.7 fusion.30
  13.9 0.1 rev.3
  14.0 0.3 fusion.20
  14.4 0.1 slice_dynamic-update-slice_fusion.13
  14.5 0.2 slice_dynamic-update-slice_fusion.12
  14.7 0.2 slice_dynamic-update-slice_fusion.11
  14.8 0.2 slice_dynamic-update-slice_fusion.10
  15.0 0.2 slice_dynamic-update-slice_fusion.9
  15.2 0.2 slice_dynamic-update-slice_fusion.8
  15.3 0.2 slice_dynamic-update-slice_fusion.7
  15.5 3.2 %fusion.33 = (bf16[16,64,896]{2,1,0:T(8,128)(2,1)S(1)}, bf16[16,64,896]{2,1,0:T(8,128)(2,1)S(1)}, bf16[16,64,896]{2,1,0:T(8,128)(2,1)S(1)}, bf16[16,64,896]{2,1,...) fusion(bf16[24,64,896]{2,1,0:T(8,128)(2,1)S(1)} %slice_dynamic-, ...), kind=kLoop, calls=%fused_computation.76 | loop fusion | bytes 33030144 | tf_op jit(solution)/shard_map/slice | solution.py:78
  18.7 0.6 fusion.37
  19.4 0.6 convolution_add_fusion.15
  20.0 0.6 convolution_add_fusion.14
  20.7 0.6 convolution_add_fusion.13
  21.3 0.6 convolution_add_fusion.12
  22.0 0.6 convolution_add_fusion.11
  22.6 0.6 convolution_add_fusion.10
  23.3 0.6 convolution_add_fusion.9
  24.0 0.7 convolution_add_fusion.8
  24.6 0.3 copy-done
  24.9 0.1 fusion.17
  25.1 1.3 %collective-permute-start.2 = (bf16[16,3,128]{2,1,0:T(4,128)(2,1)S(1)}, bf16[16,3,128]{2,1,0:T(4,128)(2,1)S(1)}, u32[]{:S(2)}, u32[]{:S(2)}) collective-permute-start(bf16[16,3,128]{2,1,0:T(4,128)(2,1)S(1)} %slice_select_fusion), channel_id=1, source_target_pairs={{0,16},{16,0},{32,48},{48,32},{64,80},{80,64},{96,112},{112,96},{1... | collective-permute-start | bytes 36872 | tf_op jit(solution)/shard_map/ppermute | solution.py:39
  26.4 0.9 fusion.8
  27.4 3.4 %collective-permute-start.4 = (bf16[4,70,128]{2,1,0:T(8,128)(2,1)S(1)}, bf16[4,70,128]{2,1,0:T(8,128)(2,1)S(1)}, u32[]{:S(2)}, u32[]{:S(2)}) collective-permute-start(bf16[4,70,128]{2,1,0:T(8,128)(2,1)S(1)} %get-tuple-element.46), channel_id=1, source_target_pairs={{1,0},{2,1},{3,2},{4,3},{5,4},{6,5},{7,6},{8,7},{9,8},{10,9},{11,1... | collective-permute-start | bytes 215048 | tf_op jit(solution)/shard_map/ppermute | solution.py:25
  30.8 2.1 %collective-permute-start.3 = (bf16[4,70,128]{2,1,0:T(8,128)(2,1)S(1)}, bf16[4,70,128]{2,1,0:T(8,128)(2,1)S(1)}, u32[]{:S(2)}, u32[]{:S(2)}) collective-permute-start(bf16[4,70,128]{2,1,0:T(8,128)(2,1)S(1)} %get-tuple-element.45), channel_id=1, source_target_pairs={{0,1},{1,2},{2,3},{3,4},{4,5},{5,6},{6,7},{7,8},{8,9},{9,10},{10,1... | collective-permute-start | bytes 215048 | tf_op jit(solution)/shard_map/ppermute | solution.py:23
  32.9 0.2 fusion.34
  33.5 4.5 %collective-permute-done.3 = bf16[4,70,128]{2,1,0:T(8,128)(2,1)S(1)} collective-permute-done((bf16[4,70,128]{2,1,0:T(8,128)(2,1)S(1)}, bf16[4,70,128]{2,1,0:T(8,128)(2,1)S(1)}, u32[]{:S(2)}, u32[]{:S(2)}) %collective-permute-start.3) | collective-permute-done | bytes 71712 | tf_op jit(solution)/shard_map/ppermute | solution.py:23
  38.0 0.1 pad_maximum_fusion
  38.1 0.1 slice_dynamic-update-slice_fusion.6
  38.2 0.2 slice_dynamic-update-slice_fusion.5
  38.4 0.2 slice_dynamic-update-slice_fusion.4
  38.6 0.2 slice_dynamic-update-slice_fusion.3
  38.7 0.2 slice_dynamic-update-slice_fusion.2
  38.9 0.2 slice_dynamic-update-slice_fusion.1
  39.1 0.2 slice_dynamic-update-slice_fusion
  39.3 3.2 %fusion.32 = (bf16[16,64,896]{2,1,0:T(8,128)(2,1)S(1)}, bf16[16,64,896]{2,1,0:T(8,128)(2,1)S(1)}, bf16[16,64,896]{2,1,0:T(8,128)(2,1)S(1)}, bf16[16,64,896]{2,1,...) fusion(bf16[24,64,896]{2,1,0:T(8,128)(2,1)S(1)} %slice_dynamic-, ...), kind=kLoop, calls=%fused_computation.75 | loop fusion | bytes 33030144 | tf_op jit(solution)/shard_map/slice | solution.py:78
  42.5 0.6 fusion.38
  43.1 0.6 convolution_add_fusion.7
  43.8 0.6 convolution_add_fusion.6
  44.4 0.6 convolution_add_fusion.5
  45.1 0.6 convolution_add_fusion.4
  45.7 0.6 convolution_add_fusion.3
  46.4 0.6 convolution_add_fusion.2
  47.0 0.6 convolution_add_fusion.1
  47.7 0.6 convolution_add_fusion
  48.3 0.9 broadcast_select_fusion
  49.2 10.2 %all-to-all-start = ((f32[16,1,64,128]{3,2,1,0:T(8,128)}), f32[16,1,64,128]{3,2,1,0:T(8,128)S(1)}, u32[]{:S(2)}, u32[]{:S(2)}) async-start(f32[16,1,64,128]{3,2,1,0:T(8,128)} %broadcast_select_fusion), calls=%async_computation | async-start | bytes 1048576 | tf_op jit(solution)/shard_map/all_to_all | solution.py:125
  59.4 17.3 %all-to-all-done = f32[16,1,64,128]{3,2,1,0:T(8,128)S(1)} async-done(((f32[16,1,64,128]{3,2,1,0:T(8,128)}), f32[16,1,64,128]{3,2,1,0:T(8,128)S(1)}, u32[]{:S(2)}, u32[]{:S(2)}) %all-to-all-start) | async-done | bytes 524320 | tf_op jit(solution)/shard_map/all_to_all | solution.py:125
  76.8 0.9 fusion.23
  77.6 0.1 concatenate.23
  77.7 31.3 %all_to_all.10 = f32[16,128,128]{2,1,0:T(8,128)S(1)} all-to-all(f32[16,128,128]{2,1,0:T(8,128)S(1)} %concatenate.23), channel_id=1, replica_groups=mesh['view'=16,'blk'=16] {'view'}, dimensions={0} | all-to-all | bytes 2097152 | tf_op jit(solution)/shard_map/all_to_all | solution.py:11
  109.0 1.0 copy.70
  (29 shorter events, 0.8 us)
Async XLA Ops:
  1.3 12.7 %collective-permute-start = (bf16[4,128,128]{2,1,0:T(8,128)(2,1)S(1)}, bf16[4,128,128]{2,1,0:T(8,128)(2,1)S(1)}, u32[]{:S(2)}, u32[]{:S(2)}) collective-permute-start(bf16[4,128,128]{2,1,0:T(8,128)(2,1)S(1)} %get-tuple-element.44), channel_id=1, source_target_pairs={{0,1},{1,2},{2,3},{3,4},{4,5},{5,6},{6,7},{7,8},{8,9},{9,10},{10,1... | collective-permute-start | bytes 393224 | tf_op jit(solution)/shard_map/ppermute | solution.py:23
  4.5 9.6 %collective-permute-start.1 = (bf16[4,128,128]{2,1,0:T(8,128)(2,1)S(1)}, bf16[4,128,128]{2,1,0:T(8,128)(2,1)S(1)}, u32[]{:S(2)}, u32[]{:S(2)}) collective-permute-start(bf16[4,128,128]{2,1,0:T(8,128)(2,1)S(1)} %get-tuple-element.43), channel_id=1, source_target_pairs={{1,0},{2,1},{3,2},{4,3},{5,4},{6,5},{7,6},{8,7},{9,8},{10,9},{11,1... | collective-permute-start | bytes 393224 | tf_op jit(solution)/shard_map/ppermute | solution.py:25
  12.2 0.7 copy-start.1
  24.0 1.0 copy-start
  25.1 2.2 %collective-permute-start.2 = (bf16[16,3,128]{2,1,0:T(4,128)(2,1)S(1)}, bf16[16,3,128]{2,1,0:T(4,128)(2,1)S(1)}, u32[]{:S(2)}, u32[]{:S(2)}) collective-permute-start(bf16[16,3,128]{2,1,0:T(4,128)(2,1)S(1)} %slice_select_fusion), channel_id=1, source_target_pairs={{0,16},{16,0},{32,48},{48,32},{64,80},{80,64},{96,112},{112,96},{1... | collective-permute-start | bytes 36872 | tf_op jit(solution)/shard_map/ppermute | solution.py:39
  27.4 6.1 %collective-permute-start.4 = (bf16[4,70,128]{2,1,0:T(8,128)(2,1)S(1)}, bf16[4,70,128]{2,1,0:T(8,128)(2,1)S(1)}, u32[]{:S(2)}, u32[]{:S(2)}) collective-permute-start(bf16[4,70,128]{2,1,0:T(8,128)(2,1)S(1)} %get-tuple-element.46), channel_id=1, source_target_pairs={{1,0},{2,1},{3,2},{4,3},{5,4},{6,5},{7,6},{8,7},{9,8},{10,9},{11,1... | collective-permute-start | bytes 215048 | tf_op jit(solution)/shard_map/ppermute | solution.py:25
  30.8 7.2 %collective-permute-start.3 = (bf16[4,70,128]{2,1,0:T(8,128)(2,1)S(1)}, bf16[4,70,128]{2,1,0:T(8,128)(2,1)S(1)}, u32[]{:S(2)}, u32[]{:S(2)}) collective-permute-start(bf16[4,70,128]{2,1,0:T(8,128)(2,1)S(1)} %get-tuple-element.45), channel_id=1, source_target_pairs={{0,1},{1,2},{2,3},{3,4},{4,5},{5,6},{6,7},{7,8},{8,9},{9,10},{10,1... | collective-permute-start | bytes 215048 | tf_op jit(solution)/shard_map/ppermute | solution.py:23
  49.2 27.5 %all-to-all-start = ((f32[16,1,64,128]{3,2,1,0:T(8,128)}), f32[16,1,64,128]{3,2,1,0:T(8,128)S(1)}, u32[]{:S(2)}, u32[]{:S(2)}) async-start(f32[16,1,64,128]{3,2,1,0:T(8,128)} %broadcast_select_fusion), calls=%async_computation | async-start | bytes 1048576 | tf_op jit(solution)/shard_map/all_to_all | solution.py:125
